TPU v7x, 256 devices: a whole 4x4x8 slice. The times are simulated.
256 devices in a mesh: dp: 128 (over x, z, y), rep: 2 (over core).
Axes of the slice: x: 4, y: 4, z: 8, core: 2. Of those that a mesh axis runs over, the one named last changes fastest.
Arguments:
- features: bfloat16 [32768, 1024], P(('dp', 'rep')), may hold values from -6 to 6
- cotangent: bfloat16 [32768, 1024], P(('dp', 'rep')), may hold values from -6 to 6
- routes: int32 [32768, 2], P(('dp', 'rep')), may hold values from 0 to 127, all different within a row; in each aligned block of 128 rows (0 to 127, 128 to 255, ...) at most 3 rows name the same one
- route_weights: float32 [32768, 2], P(('dp', 'rep')), may hold values from 0.2 to 1
- counts: int32 [32768], P(('dp', 'rep')), may hold values from 1 to 4
- cross_weight: bfloat16 [1024, 1024], P(('dp', 'rep')), may hold values from -0.1875 to 0.1875
- gate_weight: bfloat16 [1024, 1024], P(('dp', 'rep')), may hold values from -0.1875 to 0.1875
- cross_bias: float32 [1024], replicated, may hold values from -3 to 3
- gate_bias: float32 [1024], replicated, may hold values from -4 to 4
- expert_in: bfloat16 [128, 1024, 2048], P('dp', None, 'rep'), may hold values from -0.1875 to 0.1875
- expert_out: bfloat16 [128, 2048, 1024], P('dp', 'rep'), may hold values from -0.125 to 0.125
Outputs:
- layer_output: bfloat16 [32768, 1024], P(('dp', 'rep'))
- grad_cross_weight: bfloat16 [1024, 1024], P('rep')
- grad_gate_weight: bfloat16 [1024, 1024], P('rep')
- grad_cross_bias: float32 [1024], P('rep')
- grad_gate_bias: float32 [1024], P('rep')
- grad_expert_in: bfloat16 [128, 1024, 2048], P('dp', None, 'rep')
- grad_expert_out: bfloat16 [128, 2048, 1024], P('dp', 'rep')
Inputs may be any that keep to these rules, and one draw needn't show every extreme that they name: `routes`: the two experts of a row differ. In the rows of one device (aligned blocks of 128 rows) no expert is named more than 3 times, and in every draw some expert is named exactly 3 times in some block. Every expert is named by some row.
All inputs are finite; a program needn't handle non-finite values.
Results may differ from a plain program's by a relative error of at most 0.02.
Values may be sent and summed in bfloat16 or wider, within the bound.
No kernel may reach another device: no remote copies, remote signals or barrier semaphores. Data moves between devices by JAX's collectives and lax.ppermute only.
A program may use at most 128 MiB of HBM per device.

v0:
```python
import jax
import jax.numpy as jnp
from jax import lax
from jax.sharding import PartitionSpec as P


def slot_layout(routes, experts_n, capacity):
    flat_routes = routes.reshape(-1)
    onehot = (flat_routes[:, None] == jnp.arange(experts_n, dtype=jnp.int32)[None, :]).astype(
        jnp.int32
    )
    position = jnp.sum((jnp.cumsum(onehot, axis=0) - 1) * onehot, axis=1)
    slot_index = flat_routes * capacity + position
    slot_ids = jnp.arange(experts_n * capacity, dtype=jnp.int32)
    slot_match = (slot_index[None, :] == slot_ids[:, None]).astype(jnp.bfloat16)
    return (slot_index, slot_match)


def body(
    features,
    cotangent,
    routes,
    route_weights,
    counts,
    cross_weight,
    gate_weight,
    cross_bias,
    gate_bias,
    expert_in,
    expert_out,
):
    row_count, width = features.shape
    experts_n = lax.axis_size("dp")
    capacity = max(2, 3 * row_count // experts_n)
    feature_f = features.astype(jnp.float32)
    cross_acc = jnp.dot(
        features,
        lax.all_gather(cross_weight, ("dp", "rep"), axis=0, tiled=True),
        preferred_element_type=jnp.float32,
    )
    gate_acc = jnp.dot(
        features,
        lax.all_gather(gate_weight, ("dp", "rep"), axis=0, tiled=True),
        preferred_element_type=jnp.float32,
    )
    cross_term = cross_acc + cross_bias
    gate_term = jax.nn.sigmoid(gate_acc + gate_bias)
    crossed = (feature_f * cross_term * gate_term + feature_f).astype(jnp.bfloat16)
    slot_index, slot_match = slot_layout(routes, experts_n, capacity)
    row_match = jnp.sum(slot_match.reshape(experts_n * capacity, row_count, 2), axis=2)
    send_buffer = jnp.dot(row_match, crossed, preferred_element_type=jnp.float32).astype(
        jnp.bfloat16
    )
    send_buffer = send_buffer.reshape(experts_n, capacity, width)
    whole_in, whole_out = (
        lax.all_gather(expert_in, "rep", axis=2, tiled=True),
        lax.all_gather(expert_out, "rep", axis=1, tiled=True),
    )
    weight_in = whole_in[0]
    weight_out = whole_out[0]
    received = lax.all_to_all(send_buffer, "dp", split_axis=0, concat_axis=0, tiled=True)
    pre_act = jnp.einsum("skd,df->skf", received, weight_in, preferred_element_type=jnp.float32)
    hidden = (pre_act * jax.nn.sigmoid(pre_act)).astype(jnp.bfloat16)
    result = jnp.einsum("skf,fd->skd", hidden, weight_out, preferred_element_type=jnp.float32)
    expert_result, slot_inputs, pre_act, hidden = (
        result.astype(jnp.bfloat16),
        received,
        pre_act,
        hidden,
    )
    returned = lax.all_to_all(expert_result, "dp", split_axis=0, concat_axis=0, tiled=True)
    gathered_out = (
        returned.reshape(experts_n * capacity, width)[slot_index]
        .reshape(row_count, 2, width)
        .astype(jnp.float32)
    )
    layer_output = (
        crossed.astype(jnp.float32) + jnp.sum(route_weights[:, :, None] * gathered_out, axis=1)
    ).astype(jnp.bfloat16)
    upstream = 0.05 * counts.astype(jnp.float32)[:, None] * cotangent.astype(jnp.float32)
    out_grad = (
        (route_weights[:, :, None] * upstream[:, None, :])
        .astype(jnp.bfloat16)
        .reshape(2 * row_count, width)
    )
    grad_send = jnp.dot(slot_match, out_grad, preferred_element_type=jnp.float32).astype(
        jnp.bfloat16
    )
    grad_send = grad_send.reshape(experts_n, capacity, width)
    grad_recv = lax.all_to_all(grad_send, "dp", split_axis=0, concat_axis=0, tiled=True)
    squash = jax.nn.sigmoid(pre_act)
    slope = squash * (1.0 + pre_act * (1.0 - squash))
    hid_grad = jnp.einsum("skd,fd->skf", grad_recv, weight_out, preferred_element_type=jnp.float32)
    pre_grad = (hid_grad * slope).astype(jnp.bfloat16)
    back_part = jnp.einsum("skf,df->skd", pre_grad, weight_in, preferred_element_type=jnp.float32)
    back_rows = back_part.astype(jnp.bfloat16)
    returned_grad = lax.all_to_all(back_rows, "dp", split_axis=0, concat_axis=0, tiled=True)
    grad_in_full = jnp.einsum(
        "skd,skf->df", slot_inputs, pre_grad, preferred_element_type=jnp.float32
    )
    grad_out_full = jnp.einsum("skf,skd->fd", hidden, grad_recv, preferred_element_type=jnp.float32)
    grad_in_part, grad_out_part = (
        lax.psum_scatter(
            grad_in_full[None].astype(jnp.bfloat16), "rep", scatter_dimension=2, tiled=True
        ).astype(jnp.float32),
        lax.psum_scatter(
            grad_out_full[None].astype(jnp.bfloat16), "rep", scatter_dimension=1, tiled=True
        ).astype(jnp.float32),
    )
    grad_expert_in = grad_in_part.astype(jnp.bfloat16)
    grad_expert_out = grad_out_part.astype(jnp.bfloat16)
    back_gathered = (
        returned_grad.reshape(experts_n * capacity, width)[slot_index]
        .reshape(row_count, 2, width)
        .astype(jnp.float32)
    )
    crossed_grad = upstream + jnp.sum(back_gathered, axis=1)
    cross_grad = (crossed_grad * feature_f * gate_term).astype(jnp.bfloat16)
    gate_grad = (crossed_grad * feature_f * cross_term * gate_term * (1.0 - gate_term)).astype(
        jnp.bfloat16
    )
    weight_cross = jnp.einsum("rd,re->de", features, cross_grad, preferred_element_type=jnp.float32)
    weight_gate = jnp.einsum("rd,re->de", features, gate_grad, preferred_element_type=jnp.float32)
    bias_cross = jnp.sum(cross_grad.astype(jnp.float32), axis=0)
    bias_gate = jnp.sum(gate_grad.astype(jnp.float32), axis=0)
    halves = (
        lax.psum_scatter(
            weight_cross.astype(jnp.bfloat16), "rep", scatter_dimension=0, tiled=True
        ).astype(jnp.float32),
        lax.psum_scatter(
            weight_gate.astype(jnp.bfloat16), "rep", scatter_dimension=0, tiled=True
        ).astype(jnp.float32),
        lax.psum_scatter(
            bias_cross.astype(jnp.bfloat16), "rep", scatter_dimension=0, tiled=True
        ).astype(jnp.float32),
        lax.psum_scatter(
            bias_gate.astype(jnp.bfloat16), "rep", scatter_dimension=0, tiled=True
        ).astype(jnp.float32),
    )
    summed = lax.psum((halves[0], halves[1], halves[2], halves[3]), "dp")
    return (
        layer_output,
        summed[0].astype(jnp.bfloat16),
        summed[1].astype(jnp.bfloat16),
        summed[2],
        summed[3],
        grad_expert_in,
        grad_expert_out,
    )


def solution(mesh):
    return jax.shard_map(
        body,
        mesh=mesh,
        in_specs=(
            P(("dp", "rep"), None),
            P(("dp", "rep"), None),
            P(("dp", "rep"), None),
            P(("dp", "rep"), None),
            P(("dp", "rep")),
            P(("dp", "rep"), None),
            P(("dp", "rep"), None),
            P(),
            P(),
            P("dp", None, "rep"),
            P("dp", "rep", None),
        ),
        out_specs=(
            P(("dp", "rep"), None),
            P("rep", None),
            P("rep", None),
            P("rep"),
            P("rep"),
            P("dp", None, "rep"),
            P("dp", "rep", None),
        ),
        check_vma=False,
    )
```

profile of v0, /device:TPU:0, one launch (start us, length us, event | category | flops | bytes accessed | tf_op | source)
XLA Modules:
  0.0 823.5 jit_solution(13755409493693492527)
XLA Ops:
  7.2 0.7 all-gather.11.cloned.1.call-update
  8.0 0.7 all-gather.13.cloned.1.call-update
  8.7 0.7 all-gather.7.cloned.1.call-update
  11.3 105.8 %all-gather.11.cloned.1.call-done = bf16[256,4,1024]{2,1,0:T(4,128)(2,1)} async-done(((bf16[1,4,1024]{2,1,0:T(4,128)(2,1)}), bf16[256,4,1024]{2,1,0:T(4,128)(2,1)}) %all-gather.11.cloned.1.call-update) | async-done | bytes 2097168 | tf_op jit(solution)/shard_map/all_gather | solution.py:38
  117.1 2.5 reshape.133
  119.7 104.3 %all-gather.13.cloned.1.call-done = bf16[256,4,1024]{2,1,0:T(4,128)(2,1)} async-done(((bf16[1,4,1024]{2,1,0:T(4,128)(2,1)}), bf16[256,4,1024]{2,1,0:T(4,128)(2,1)}) %all-gather.13.cloned.1.call-update) | async-done | bytes 2097168 | tf_op jit(solution)/shard_map/all_gather | solution.py:43
  223.9 3.9 reshape.135
  228.4 3.1 fusion.25
  231.8 1.3 reshape.110
  233.1 11.8 %all-to-all-start = ((bf16[128,3,1024]{2,1,0:T(4,128)(2,1)}), bf16[128,3,1024]{2,1,0:T(4,128)(2,1)S(1)}, u32[]{:S(2)}, u32[]{:S(2)}) async-start(bf16[128,3,1024]{2,1,0:T(4,128)(2,1)} %reshape.110), calls=%async_computation | async-start | bytes 2097152 | tf_op jit(solution)/shard_map/all_to_all | solution.py:61
  245.6 0.7 mul.121
  246.9 1.3 reshape.112
  248.2 27.1 %all-to-all-done = bf16[128,3,1024]{2,1,0:T(4,128)(2,1)S(1)} async-done(((bf16[128,3,1024]{2,1,0:T(4,128)(2,1)}), bf16[128,3,1024]{2,1,0:T(4,128)(2,1)S(1)}, u32[]{:S(2)}, u32[]{:S(2)}) %all-to-all-start) | async-done | bytes 786464 | tf_op jit(solution)/shard_map/all_to_all | solution.py:61
  275.3 7.9 all-to-all-start.2
  283.2 0.8 copy.69
  284.1 5.7 fusion.6
  289.8 22.5 %all-to-all-done.2 = bf16[128,3,1024]{2,1,0:T(4,128)(2,1)} async-done(((bf16[128,3,1024]{2,1,0:T(4,128)(2,1)}), bf16[128,3,1024]{2,1,0:T(4,128)(2,1)}, u32[]{:S(2)}, u32[]{:S(2)}) %all-to-all-start.2) | async-done | bytes 786464 | tf_op jit(solution)/shard_map/all_to_all | solution.py:90
  312.3 5.9 multiply_convert_fusion
  318.3 1.8 fusion.12
  320.1 1.6 copy.68
  321.8 7.0 all-to-all-start.3
  329.2 28.5 %all-to-all-done.3 = bf16[128,3,1024]{2,1,0:T(4,128)(2,1)S(1)} async-done(((bf16[128,3,1024]{2,1,0:T(4,128)(2,1)}), bf16[128,3,1024]{2,1,0:T(4,128)(2,1)S(1)}, u32[]{:S(2)}, u32[]{:S(2)}) %all-to-all-start.3) | async-done | bytes 786464 | tf_op jit(solution)/shard_map/all_to_all | solution.py:97
  357.7 0.7 reshape.113
  358.4 1.2 gather_fusion.1
  359.5 0.7 reshape.115
  360.2 1.2 reduce_sum.72
  361.5 1.4 fusion.35
  362.9 2.1 convert_bitcast_fusion.1
  365.0 2.1 convert_bitcast_fusion
  367.2 7.6 reduce-scatter.5.cloned.1.call-done
  374.7 19.3 %reduce-scatter.7.cloned.1.call-done = bf16[512,1024]{0,1:T(8,128)(2,1)} async-done(((bf16[1024,1024]{0,1:T(8,128)(2,1)}), bf16[512,1024]{0,1:T(8,128)(2,1)}) %reduce-scatter.7.cloned.1.call-update) | async-done | bytes 1048592 | tf_op jit(solution)/shard_map/reduce_scatter | solution.py:130
  394.1 3.9 fusion.8
  398.1 1.8 copy-done.2
  399.9 5.8 fusion.9
  405.7 4.0 fusion.15
  409.7 1.6 copy.65
  411.4 13.9 %all-to-all-start.1 = ((bf16[128,3,1024]{2,1,0:T(4,128)(2,1)}), bf16[128,3,1024]{2,1,0:T(4,128)(2,1)S(1)}, u32[]{:S(2)}, u32[]{:S(2)}) async-start(bf16[128,3,1024]{2,1,0:T(4,128)(2,1)} %copy.65), calls=%async_computation.1 | async-start | bytes 2097152 | tf_op jit(solution)/shard_map/all_to_all | solution.py:71
  425.3 0.6 dynamic-slice
  426.5 33.4 %all-to-all-done.1 = bf16[128,3,1024]{2,1,0:T(4,128)(2,1)S(1)} async-done(((bf16[128,3,1024]{2,1,0:T(4,128)(2,1)}), bf16[128,3,1024]{2,1,0:T(4,128)(2,1)S(1)}, u32[]{:S(2)}, u32[]{:S(2)}) %all-to-all-start.1) | async-done | bytes 786464 | tf_op jit(solution)/shard_map/all_to_all | solution.py:71
  459.9 0.7 reshape.111
  460.6 1.2 gather_fusion
  461.8 0.7 reshape.114
  462.5 2.5 all-reduce.4
  465.0 345.2 %all-reduce.2 = (f32[512]{0:T(512)}, f32[512]{0:T(512)}) all-reduce(f32[512]{0:T(512)S(1)} %get-tuple-element.52, f32[512]{0:T(512)S(1)} %get-tuple-element.51), channel_id=1, replica_groups=mesh['dp'=128,'rep'=2] {'dp'}, use_global_device_ids=true, to_apply=%region_12.13 | all-reduce | flops 1024 | bytes 8192 | tf_op jit(solution)/shard_map/psum | solution.py:140
  810.2 1.3 multiply_reduce_fusion
  811.6 0.8 add_convert_fusion
  812.4 2.3 copy.72
  814.7 2.3 copy.73
  (79 shorter events, 4.8 us)
Async XLA Ops:
  7.2 2.8 copy-start.9
  7.2 109.9 %all-gather.11.cloned.1.call-start = ((), (), s32[]{:S(2)}) async-start(), calls=%async_computation.14 | async-start | bytes 2105344 | tf_op jit(solution)/shard_map/all_gather | solution.py:38
  7.9 216.0 %all-gather.13.cloned.1.call-start = ((), (), s32[]{:S(2)}) async-start(), calls=%async_computation.15 | async-start | bytes 2105344 | tf_op jit(solution)/shard_map/all_gather | solution.py:43
  8.7 275.4 %all-gather.7.cloned.1.call-start = ((), (), s32[]{:S(2)}) async-start(), calls=%async_computation.8 | async-start | bytes 6291456 | tf_op jit(solution)/shard_map/all_gather | solution.py:56
  9.4 302.9 %all-gather.9.cloned.1.call-start = ((), (), s32[]{:S(2)}) async-start(), calls=%async_computation.9 | async-start | bytes 6291456 | tf_op jit(solution)/shard_map/all_gather | solution.py:57
  119.6 108.3 %copy-start.1 = (bf16[128,1024]{1,0:T(8,128)(2,1)S(1)}, bf16[128,1024]{1,0:T(8,128)(2,1)}, u32[]{:S(2)}) copy-start(bf16[128,1024]{1,0:T(8,128)(2,1)} %param.11) | copy-start | bytes 786436
  119.6 108.2 %copy-start.8 = (f32[1024]{0:T(1024)S(1)}, f32[1024]{0:T(1024)}, u32[]{:S(2)}) copy-start(f32[1024]{0:T(1024)} %param.18) | copy-start | bytes 12292
  119.6 108.7 %copy-start.11 = (f32[1024]{0:T(1024)S(1)}, f32[1024]{0:T(1024)}, u32[]{:S(2)}) copy-start(f32[1024]{0:T(1024)} %param.19) | copy-start | bytes 12292
  228.3 4.8 copy-start.3
  231.5 13.8 %copy-start.6 = (bf16[128,1024]{1,0:T(8,128)(2,1)}, bf16[128,1024]{1,0:T(8,128)(2,1)S(1)}, u32[]{:S(2)}) copy-start(bf16[128,1024]{1,0:T(8,128)(2,1)S(1)} %get-tuple-element.49) | copy-start | bytes 786436
  231.5 13.5 %copy-start.10 = (f32[128,2]{0,1:T(2,128)S(1)}, f32[128,2]{0,1:T(2,128)}, u32[]{:S(2)}) copy-start(f32[128,2]{0,1:T(2,128)} %param.14) | copy-start | bytes 3076
  231.5 13.6 %copy-start.12 = (s32[128]{0:T(128)S(1)}, s32[128]{0:T(128)}, u32[]{:S(2)}) copy-start(s32[128]{0:T(128)} %param.15) | copy-start | bytes 1540
  231.5 13.6 %copy-start.5 = (bf16[128,1024]{1,0:T(8,128)(2,1)S(1)}, bf16[128,1024]{1,0:T(8,128)(2,1)}, u32[]{:S(2)}) copy-start(bf16[128,1024]{1,0:T(8,128)(2,1)} %param.12) | copy-start | bytes 786436
  233.1 42.2 %all-to-all-start = ((bf16[128,3,1024]{2,1,0:T(4,128)(2,1)}), bf16[128,3,1024]{2,1,0:T(4,128)(2,1)S(1)}, u32[]{:S(2)}, u32[]{:S(2)}) async-start(bf16[128,3,1024]{2,1,0:T(4,128)(2,1)} %reshape.110), calls=%async_computation | async-start | bytes 2097152 | tf_op jit(solution)/shard_map/all_to_all | solution.py:61
  275.3 37.0 %all-to-all-start.2 = ((bf16[128,3,1024]{2,1,0:T(4,128)(2,1)}), bf16[128,3,1024]{2,1,0:T(4,128)(2,1)}, u32[]{:S(2)}, u32[]{:S(2)}) async-start(bf16[128,3,1024]{2,1,0:T(4,128)(2,1)} %reshape.112), calls=%async_computation.2 | async-start | bytes 2097152 | tf_op jit(solution)/shard_map/all_to_all | solution.py:90
  312.3 5.9 copy-start
  318.3 1.8 copy-start.14
  321.8 35.9 %all-to-all-start.3 = ((bf16[128,3,1024]{2,1,0:T(4,128)(2,1)}), bf16[128,3,1024]{2,1,0:T(4,128)(2,1)S(1)}, u32[]{:S(2)}, u32[]{:S(2)}) async-start(bf16[128,3,1024]{2,1,0:T(4,128)(2,1)} %copy.68), calls=%async_computation.3 | async-start | bytes 2097152 | tf_op jit(solution)/shard_map/all_to_all | solution.py:97
  328.7 46.0 %reduce-scatter.5.cloned.1.call-start = ((), (), s32[]{:S(2)}) async-start(), calls=%async_computation.10 | async-start | bytes 3145728 | tf_op jit(solution)/shard_map/reduce_scatter | solution.py:127
  358.4 3.1 copy-start.4
  365.0 29.0 %reduce-scatter.7.cloned.1.call-start = ((), (), s32[]{:S(2)}) async-start(), calls=%async_computation.11 | async-start | bytes 3145728 | tf_op jit(solution)/shard_map/reduce_scatter | solution.py:130
  365.0 29.1 %copy-start.15 = (bf16[128,3,2048]{2,0,1:T(8,128)(2,1)S(1)}, bf16[128,3,2048]{2,0,1:T(8,128)(2,1)}, u32[]{:S(2)}) copy-start(bf16[128,3,2048]{2,0,1:T(8,128)(2,1)} %copy-done.14) | copy-start | bytes 4718596
  367.1 445.3 %all-reduce.7.cloned.1.call-start = ((), (), s32[]{:S(2)}) async-start(), calls=%async_computation.16 | async-start | bytes 4194304 | tf_op jit(solution)/shard_map/psum | solution.py:140
  394.0 422.9 %reduce-scatter.9.cloned.1.call-start = ((), (), s32[]{:S(2)}) async-start(), calls=%async_computation.12 | async-start | bytes 6291456 | tf_op jit(solution)/shard_map/reduce_scatter | solution.py:103
  398.0 1.9 copy-start.2
  398.0 418.9 %reduce-scatter.11.cloned.1.call-start = ((), (), s32[]{:S(2)}) async-start(), calls=%async_computation.13 | async-start | bytes 6291456 | tf_op jit(solution)/shard_map/reduce_scatter | solution.py:106
  409.7 15.5 %copy-start.13 = (u32[256]{0:T(256)S(1)}, u32[256]{0:T(256)}, u32[]{:S(2)}) copy-start(u32[256]{0:T(256)} %constant.36) | copy-start | bytes 3076
  411.4 48.5 %all-to-all-start.1 = ((bf16[128,3,1024]{2,1,0:T(4,128)(2,1)}), bf16[128,3,1024]{2,1,0:T(4,128)(2,1)S(1)}, u32[]{:S(2)}, u32[]{:S(2)}) async-start(bf16[128,3,1024]{2,1,0:T(4,128)(2,1)} %copy.65), calls=%async_computation.1 | async-start | bytes 2097152 | tf_op jit(solution)/shard_map/all_to_all | solution.py:71
  460.6 351.0 %copy-start.7 = (bf16[128,1024]{1,0:T(8,128)(2,1)S(1)}, bf16[128,1024]{1,0:T(8,128)(2,1)}, u32[]{:S(2)}) copy-start(bf16[128,1024]{1,0:T(8,128)(2,1)} %copy-done.6) | copy-start | bytes 786436
Sparse Core Ops, SparseCore 0:
  11.7 105.3 all-gather.10
  120.8 103.0 all-gather.12
  225.7 18.2 all-gather.6
  245.7 20.2 all-gather.8
  365.1 9.5 reduce-scatter.4
  377.6 16.3 reduce-scatter.6
  399.6 236.3 all-reduce.6
  639.1 14.6 reduce-scatter.8
  657.0 18.7 reduce-scatter.10
where the time goes:
time: 824 us; the launch traced here: 823 us
  waiting for transfers between devices  351 us (43%)
  blocking collectives  348 us (42%)
  starting transfers between devices  41.2 us (5%)
  matrix products  35.6 us (4%)
  local copies, waits for them, and re-layouts  27.4 us (3%)
  between operations  14.9 us (2%)
    psum x1, blocking collectives, body(): summed = lax.psum((halves[0], halves[1], halves[2], halves[3]), 'dp')  345 us
    all_gather x1, waiting for transfers between devices, body(): lax.all_gather(cross_weight, ('dp', 'rep'), axis=0, tiled=True)  106 us
    all_gather x1, waiting for transfers between devices, body(): lax.all_gather(gate_weight, ('dp', 'rep'), axis=0, tiled=True)  104 us
    all_to_all x1, waiting for transfers between devices, body(): lax.all_to_all(expert_result, 'dp', split_axis=0, concat_axis=0, tiled=True)  33.4 us
    all_to_all x1, waiting for transfers between devices, body(): lax.all_to_all(back_rows, 'dp', split_axis=0, concat_axis=0, tiled=True)  28.5 us
    all_to_all x1, waiting for transfers between devices, body(): lax.all_to_all(send_buffer, 'dp', split_axis=0, concat_axis=0, tiled=True)  27.1 us
    all_to_all x1, waiting for transfers between devices, body(): lax.all_to_all(grad_send, 'dp', split_axis=0, concat_axis=0, tiled=True)  22.5 us
    reduce_scatter x1, waiting for transfers between devices, body(): lax.psum_scatter(weight_gate.astype(jnp.bfloat16), 'rep', scatter_dimensi...  19.3 us
  transfers between devices with their start and end apart: 13, of which 8 were waited for; matrix products, arithmetic and copies ran while one was open for 6% of the time, Pallas kernels for 0%

commit v1 on v0

--- a/solution.py
+++ b/solution.py
@@ -2,6 +2,11 @@
 import jax.numpy as jnp
 from jax import lax
 from jax.sharding import PartitionSpec as P
+
+
+def all_by_exchange(x, name, dim):
+    stack = jnp.stack([x] * lax.axis_size(name))
+    return jnp.concatenate(lax.all_to_all(stack, name, 0, 0), axis=dim)
 
 
 def slot_layout(routes, experts_n, capacity):
@@ -39,9 +44,7 @@
         preferred_element_type=jnp.float32,
     )
     gate_acc = jnp.dot(
-        features,
-        lax.all_gather(gate_weight, ("dp", "rep"), axis=0, tiled=True),
-        preferred_element_type=jnp.float32,
+        features, all_by_exchange(gate_weight, ("dp", "rep"), 0), preferred_element_type=jnp.float32
     )
     cross_term = cross_acc + cross_bias
     gate_term = jax.nn.sigmoid(gate_acc + gate_bias)

time: 824 us -> 726 us (0.88)
  waiting for transfers between devices: 351 us -> 234 us
  starting transfers between devices: 41.2 us -> 55.7 us
    all_gather x1 -> x0, waiting for transfers between devices: 104 us -> none  [body(): lax.all_gather(gate_weight, ('dp', 'rep'), axis=0, tiled=True)]
    all_to_all x0 -> x1, starting transfers between devices: none -> 14.6 us  [all_by_exchange(): return jnp.concatenate(lax.all_to_all(stack, name, 0, 0), axis=dim)]
    all_gather x1, waiting for transfers between devices: 106 us -> 93.3 us  [body(): lax.all_gather(cross_weight, ('dp', 'rep'), axis=0, tiled=True)]
  transfers between devices with their start and end apart: 13 -> 13, of which waited for: 8 -> 7; matrix products, arithmetic and copies ran while one was open for 6% -> 7% of each run, Pallas kernels for 0% -> 0%
where the time goes in v1:
time: 726 us; the launch traced here: 725 us
  blocking collectives  347 us (48%)
  waiting for transfers between devices  234 us (32%)
  starting transfers between devices  55.7 us (8%)
  matrix products  37.2 us (5%)
  local copies, waits for them, and re-layouts  29.4 us (4%)
  between operations  15.2 us (2%)
    psum x1, blocking collectives, body(): summed = lax.psum((halves[0], halves[1], halves[2], halves[3]), 'dp')  345 us
    all_gather x1, waiting for transfers between devices, body(): lax.all_gather(cross_weight, ('dp', 'rep'), axis=0, tiled=True)  93.3 us
    all_to_all x1, waiting for transfers between devices, body(): lax.all_to_all(expert_result, 'dp', split_axis=0, concat_axis=0, tiled=True)  33.7 us
    all_to_all x1, waiting for transfers between devices, body(): lax.all_to_all(back_rows, 'dp', split_axis=0, concat_axis=0, tiled=True)  28.5 us
    all_to_all x1, waiting for transfers between devices, body(): lax.all_to_all(send_buffer, 'dp', split_axis=0, concat_axis=0, tiled=True)  27.1 us
    all_to_all x1, waiting for transfers between devices, body(): lax.all_to_all(grad_send, 'dp', split_axis=0, concat_axis=0, tiled=True)  22.5 us
    reduce_scatter x1, waiting for transfers between devices, body(): lax.psum_scatter(weight_gate.astype(jnp.bfloat16), 'rep', scatter_dimensi...  19.3 us
    all_to_all x1, starting transfers between devices, all_by_exchange(): return jnp.concatenate(lax.all_to_all(stack, name, 0, 0), axis=dim)  14.6 us
  transfers between devices with their start and end apart: 13, of which 7 were waited for; matrix products, arithmetic and copies ran while one was open for 7% of the time, Pallas kernels for 0%

profile of v1, /device:TPU:0, one launch (start us, length us, event | category | flops | bytes accessed | tf_op | source)
XLA Modules:
  0.0 724.5 jit_solution(18181867013735243908)
XLA Ops:
  7.2 0.7 all-gather.9.cloned.1.call-update
  7.9 0.7 all-gather.5.cloned.1.call-update
  8.6 2.6 stack.2
  11.2 14.6 %all-to-all-start = ((bf16[256,4,1024]{2,1,0:T(4,128)(2,1)}), bf16[256,4,1024]{2,1,0:T(4,128)(2,1)S(1)}, u32[]{:S(2)}, u32[]{:S(2)}) async-start(bf16[256,4,1024]{2,1,0:T(4,128)(2,1)} %stack.2), calls=%async_computation | async-start | bytes 4194304 | tf_op jit(solution)/shard_map/all_to_all | solution.py:9
  25.9 0.7 all-gather.7.cloned.1.call-update
  27.9 93.3 %all-gather.9.cloned.1.call-done = bf16[256,4,1024]{2,1,0:T(4,128)(2,1)} async-done(((bf16[1,4,1024]{2,1,0:T(4,128)(2,1)}), bf16[256,4,1024]{2,1,0:T(4,128)(2,1)}) %all-gather.9.cloned.1.call-update) | async-done | bytes 2097168 | tf_op jit(solution)/shard_map/all_gather | solution.py:43
  121.2 3.9 reshape.139
  125.1 2.0 reshape.114
  127.2 2.0 convolution_add_fusion.1
  129.2 3.1 fusion.25
  132.7 1.3 reshape.116
  134.0 11.8 %all-to-all-start.1 = ((bf16[128,3,1024]{2,1,0:T(4,128)(2,1)}), bf16[128,3,1024]{2,1,0:T(4,128)(2,1)S(1)}, u32[]{:S(2)}, u32[]{:S(2)}) async-start(bf16[128,3,1024]{2,1,0:T(4,128)(2,1)} %reshape.116), calls=%async_computation.1 | async-start | bytes 2097152 | tf_op jit(solution)/shard_map/all_to_all | solution.py:64
  146.5 0.7 mul.121
  147.8 1.3 reshape.118
  149.1 27.1 %all-to-all-done.1 = bf16[128,3,1024]{2,1,0:T(4,128)(2,1)S(1)} async-done(((bf16[128,3,1024]{2,1,0:T(4,128)(2,1)}), bf16[128,3,1024]{2,1,0:T(4,128)(2,1)S(1)}, u32[]{:S(2)}, u32[]{:S(2)}) %all-to-all-start.1) | async-done | bytes 786464 | tf_op jit(solution)/shard_map/all_to_all | solution.py:64
  176.2 7.9 %all-to-all-start.3 = ((bf16[128,3,1024]{2,1,0:T(4,128)(2,1)}), bf16[128,3,1024]{2,1,0:T(4,128)(2,1)}, u32[]{:S(2)}, u32[]{:S(2)}) async-start(bf16[128,3,1024]{2,1,0:T(4,128)(2,1)} %reshape.118), calls=%async_computation.3 | async-start | bytes 2097152 | tf_op jit(solution)/shard_map/all_to_all | solution.py:93
  184.1 0.8 copy.69
  185.0 5.7 fusion.6
  190.7 22.5 %all-to-all-done.3 = bf16[128,3,1024]{2,1,0:T(4,128)(2,1)} async-done(((bf16[128,3,1024]{2,1,0:T(4,128)(2,1)}), bf16[128,3,1024]{2,1,0:T(4,128)(2,1)}, u32[]{:S(2)}, u32[]{:S(2)}) %all-to-all-start.3) | async-done | bytes 786464 | tf_op jit(solution)/shard_map/all_to_all | solution.py:93
  213.2 5.9 multiply_convert_fusion
  219.1 1.8 fusion.12
  221.0 1.6 copy.68
  222.6 7.0 all-to-all-start.4
  230.0 28.5 %all-to-all-done.4 = bf16[128,3,1024]{2,1,0:T(4,128)(2,1)S(1)} async-done(((bf16[128,3,1024]{2,1,0:T(4,128)(2,1)}), bf16[128,3,1024]{2,1,0:T(4,128)(2,1)S(1)}, u32[]{:S(2)}, u32[]{:S(2)}) %all-to-all-start.4) | async-done | bytes 786464 | tf_op jit(solution)/shard_map/all_to_all | solution.py:100
  258.5 0.7 reshape.119
  259.2 1.2 gather_fusion.1
  260.4 0.7 reshape.121
  261.1 1.2 reduce_sum.72
  262.3 1.4 fusion.35
  263.8 2.1 convert_bitcast_fusion.1
  265.9 2.1 convert_bitcast_fusion
  268.0 7.6 %reduce-scatter.5.cloned.1.call-done = bf16[512,1024]{0,1:T(8,128)(2,1)} async-done(((bf16[1024,1024]{0,1:T(8,128)(2,1)}), bf16[512,1024]{0,1:T(8,128)(2,1)}) %reduce-scatter.5.cloned.1.call-update) | async-done | bytes 1048592 | tf_op jit(solution)/shard_map/reduce_scatter | solution.py:130
  275.6 19.3 %reduce-scatter.7.cloned.1.call-done = bf16[512,1024]{0,1:T(8,128)(2,1)} async-done(((bf16[1024,1024]{0,1:T(8,128)(2,1)}), bf16[512,1024]{0,1:T(8,128)(2,1)}) %reduce-scatter.7.cloned.1.call-update) | async-done | bytes 1048592 | tf_op jit(solution)/shard_map/reduce_scatter | solution.py:133
  295.0 3.9 fusion.8
  298.9 1.8 copy-done.2
  300.8 5.8 fusion.9
  306.6 4.0 fusion.15
  310.6 1.6 copy.65
  312.3 13.8 %all-to-all-start.2 = ((bf16[128,3,1024]{2,1,0:T(4,128)(2,1)}), bf16[128,3,1024]{2,1,0:T(4,128)(2,1)S(1)}, u32[]{:S(2)}, u32[]{:S(2)}) async-start(bf16[128,3,1024]{2,1,0:T(4,128)(2,1)} %copy.65), calls=%async_computation.2 | async-start | bytes 2097152 | tf_op jit(solution)/shard_map/all_to_all | solution.py:74
  327.4 33.7 %all-to-all-done.2 = bf16[128,3,1024]{2,1,0:T(4,128)(2,1)S(1)} async-done(((bf16[128,3,1024]{2,1,0:T(4,128)(2,1)}), bf16[128,3,1024]{2,1,0:T(4,128)(2,1)S(1)}, u32[]{:S(2)}, u32[]{:S(2)}) %all-to-all-start.2) | async-done | bytes 786464 | tf_op jit(solution)/shard_map/all_to_all | solution.py:74
  361.0 0.7 reshape.117
  361.7 1.2 gather_fusion
  363.5 2.5 all-reduce.4
  366.1 344.9 %all-reduce.2 = (f32[512]{0:T(512)}, f32[512]{0:T(512)}) all-reduce(f32[512]{0:T(512)S(1)} %get-tuple-element.52, f32[512]{0:T(512)S(1)} %get-tuple-element.51), channel_id=1, replica_groups=mesh['dp'=128,'rep'=2] {'dp'}, use_global_device_ids=true, to_apply=%region_12.13 | all-reduce | flops 1024 | bytes 8192 | tf_op jit(solution)/shard_map/psum | solution.py:143
  711.0 1.3 multiply_reduce_fusion
  712.4 0.8 add_convert_fusion
  713.2 2.3 copy.72
  715.4 2.3 copy.73
  (79 shorter events, 5.0 us)
Async XLA Ops:
  7.2 114.0 %all-gather.9.cloned.1.call-start = ((), (), s32[]{:S(2)}) async-start(), calls=%async_computation.15 | async-start | bytes 2105344 | tf_op jit(solution)/shard_map/all_gather | solution.py:43
  7.9 177.1 %all-gather.5.cloned.1.call-start = ((), (), s32[]{:S(2)}) async-start(), calls=%async_computation.9 | async-start | bytes 6291456 | tf_op jit(solution)/shard_map/all_gather | solution.py:59
  11.2 15.3 %copy-start.9 = (s32[128,2]{0,1:T(2,128)S(1)}, s32[128,2]{0,1:T(2,128)}, u32[]{:S(2)}) copy-start(s32[128,2]{0,1:T(2,128)} %param.13) | copy-start | bytes 3076
  11.2 113.9 %all-to-all-start = ((bf16[256,4,1024]{2,1,0:T(4,128)(2,1)}), bf16[256,4,1024]{2,1,0:T(4,128)(2,1)S(1)}, u32[]{:S(2)}, u32[]{:S(2)}) async-start(bf16[256,4,1024]{2,1,0:T(4,128)(2,1)} %stack.2), calls=%async_computation | async-start | bytes 4194304 | tf_op jit(solution)/shard_map/all_to_all | solution.py:9
  25.8 187.4 %all-gather.7.cloned.1.call-start = ((), (), s32[]{:S(2)}) async-start(), calls=%async_computation.10 | async-start | bytes 6291456 | tf_op jit(solution)/shard_map/all_gather | solution.py:60
  27.9 99.2 %copy-start.1 = (bf16[128,1024]{1,0:T(8,128)(2,1)S(1)}, bf16[128,1024]{1,0:T(8,128)(2,1)}, u32[]{:S(2)}) copy-start(bf16[128,1024]{1,0:T(8,128)(2,1)} %param.11) | copy-start | bytes 786436
  27.9 99.2 %copy-start.8 = (f32[1024]{0:T(1024)S(1)}, f32[1024]{0:T(1024)}, u32[]{:S(2)}) copy-start(f32[1024]{0:T(1024)} %param.18) | copy-start | bytes 12292
  125.1 4.1 copy-start.11
  129.2 3.1 copy-start.3
  132.3 1.7 copy-start.6
  132.3 13.5 %copy-start.10 = (f32[128,2]{0,1:T(2,128)S(1)}, f32[128,2]{0,1:T(2,128)}, u32[]{:S(2)}) copy-start(f32[128,2]{0,1:T(2,128)} %param.14) | copy-start | bytes 3076
  132.3 13.6 %copy-start.12 = (s32[128]{0:T(128)S(1)}, s32[128]{0:T(128)}, u32[]{:S(2)}) copy-start(s32[128]{0:T(128)} %param.15) | copy-start | bytes 1540
  132.3 13.6 %copy-start.5 = (bf16[128,1024]{1,0:T(8,128)(2,1)S(1)}, bf16[128,1024]{1,0:T(8,128)(2,1)}, u32[]{:S(2)}) copy-start(bf16[128,1024]{1,0:T(8,128)(2,1)} %param.12) | copy-start | bytes 786436
  134.0 42.2 %all-to-all-start.1 = ((bf16[128,3,1024]{2,1,0:T(4,128)(2,1)}), bf16[128,3,1024]{2,1,0:T(4,128)(2,1)S(1)}, u32[]{:S(2)}, u32[]{:S(2)}) async-start(bf16[128,3,1024]{2,1,0:T(4,128)(2,1)} %reshape.116), calls=%async_computation.1 | async-start | bytes 2097152 | tf_op jit(solution)/shard_map/all_to_all | solution.py:64
  176.2 37.0 %all-to-all-start.3 = ((bf16[128,3,1024]{2,1,0:T(4,128)(2,1)}), bf16[128,3,1024]{2,1,0:T(4,128)(2,1)}, u32[]{:S(2)}, u32[]{:S(2)}) async-start(bf16[128,3,1024]{2,1,0:T(4,128)(2,1)} %reshape.118), calls=%async_computation.3 | async-start | bytes 2097152 | tf_op jit(solution)/shard_map/all_to_all | solution.py:93
  213.2 5.9 copy-start
  219.1 1.8 copy-start.14
  222.6 35.9 %all-to-all-start.4 = ((bf16[128,3,1024]{2,1,0:T(4,128)(2,1)}), bf16[128,3,1024]{2,1,0:T(4,128)(2,1)S(1)}, u32[]{:S(2)}, u32[]{:S(2)}) async-start(bf16[128,3,1024]{2,1,0:T(4,128)(2,1)} %copy.68), calls=%async_computation.4 | async-start | bytes 2097152 | tf_op jit(solution)/shard_map/all_to_all | solution.py:100
  229.6 46.0 %reduce-scatter.5.cloned.1.call-start = ((), (), s32[]{:S(2)}) async-start(), calls=%async_computation.11 | async-start | bytes 3145728 | tf_op jit(solution)/shard_map/reduce_scatter | solution.py:130
  259.2 3.1 copy-start.4
  265.8 29.0 %reduce-scatter.7.cloned.1.call-start = ((), (), s32[]{:S(2)}) async-start(), calls=%async_computation.12 | async-start | bytes 3145728 | tf_op jit(solution)/shard_map/reduce_scatter | solution.py:133
  265.9 29.1 %copy-start.15 = (bf16[128,3,2048]{2,0,1:T(8,128)(2,1)S(1)}, bf16[128,3,2048]{2,0,1:T(8,128)(2,1)}, u32[]{:S(2)}) copy-start(bf16[128,3,2048]{2,0,1:T(8,128)(2,1)} %copy-done.14) | copy-start | bytes 4718596
  268.0 445.2 %all-reduce.7.cloned.1.call-start = ((), (), s32[]{:S(2)}) async-start(), calls=%async_computation.16 | async-start | bytes 4194304 | tf_op jit(solution)/shard_map/psum | solution.py:143
  294.9 422.8 %reduce-scatter.9.cloned.1.call-start = ((), (), s32[]{:S(2)}) async-start(), calls=%async_computation.13 | async-start | bytes 6291456 | tf_op jit(solution)/shard_map/reduce_scatter | solution.py:106
  298.9 1.9 copy-start.2
  298.9 418.8 %reduce-scatter.11.cloned.1.call-start = ((), (), s32[]{:S(2)}) async-start(), calls=%async_computation.14 | async-start | bytes 6291456 | tf_op jit(solution)/shard_map/reduce_scatter | solution.py:109
  310.6 15.5 %copy-start.13 = (u32[256]{0:T(256)S(1)}, u32[256]{0:T(256)}, u32[]{:S(2)}) copy-start(u32[256]{0:T(256)} %constant.36) | copy-start | bytes 3076
  312.3 48.8 %all-to-all-start.2 = ((bf16[128,3,1024]{2,1,0:T(4,128)(2,1)}), bf16[128,3,1024]{2,1,0:T(4,128)(2,1)S(1)}, u32[]{:S(2)}, u32[]{:S(2)}) async-start(bf16[128,3,1024]{2,1,0:T(4,128)(2,1)} %copy.65), calls=%async_computation.2 | async-start | bytes 2097152 | tf_op jit(solution)/shard_map/all_to_all | solution.py:74
  361.7 350.7 %copy-start.7 = (bf16[128,1024]{1,0:T(8,128)(2,1)S(1)}, bf16[128,1024]{1,0:T(8,128)(2,1)}, u32[]{:S(2)}) copy-start(bf16[128,1024]{1,0:T(8,128)(2,1)} %copy-done.6) | copy-start | bytes 786436
Sparse Core Ops, SparseCore 0:
  11.7 109.4 all-gather.8
  123.0 18.2 all-gather.4
  143.1 20.2 all-gather.6
  266.0 9.5 reduce-scatter.4
  278.5 16.3 reduce-scatter.6
  300.3 235.9 all-reduce.6
  539.5 14.7 reduce-scatter.8
  557.4 18.7 reduce-scatter.10
